TPU v7x, 256 devices: a whole 4x4x8 slice. The times are simulated.
256 devices in a mesh: dp: 4 (over x), seq: 64 (over z, y, core).
Axes of the slice: x: 4, y: 4, z: 8, core: 2. Of those that a mesh axis runs over, the one named last changes fastest.
Arguments:
- streams: bfloat16 [3, 4, 8192, 4096], P(None, 'dp', 'seq'), may hold values from -6 to 6
- short_filter: float32 [3, 3, 4096], P(None, None, 'dp'), may hold values from -3.5 to 3.5
- decay_rate: float32 [2, 4096], P(None, 'dp'), may hold values from 1.2207031e-06 to 0.05
- pole_angle: float32 [2, 4096], P(None, 'dp'), may hold values from -3.140625 to 3.140625
- residue_re: float32 [2, 4096], P(None, 'dp'), may hold values from -6 to 6
- residue_im: float32 [2, 4096], P(None, 'dp'), may hold values from -6 to 6
- skip_gain: float32 [4096], P('dp'), may hold values from -6 to 6
- doc_starts: int32 [4, 8], P('dp'), may hold values from 0 to 8191, as said below
Outputs:
- mixed: bfloat16 [4, 8192, 4096], P('dp', 'seq')
Inputs may be any that keep to these rules, and one draw needn't show every extreme that they name: `doc_starts`: each row starts with 0 and rises strictly; the last document of every sequence is one position long.
All inputs are finite; a program needn't handle non-finite values.
Results may differ from a plain program's by a relative error of at most 0.0045.
Values may be sent and summed in bfloat16 or wider, within the bound.
A program may use at most 128 MiB of HBM per device.

v0:
```python
import jax
import jax.numpy as jnp
from jax import lax
from jax.sharding import PartitionSpec as P

block_len = 32


def from_behind(x, axis, by):
    count = lax.axis_size(axis)
    pairs = [(i, i + by) for i in range(count) if 0 <= i + by < count]
    return lax.ppermute(x, axis, pairs)


def prefix_2(part, axis, combine, identity):
    place = lax.axis_index(axis)
    gathered = jax.tree.map(lambda a: lax.all_gather(a, axis), part)
    state = jax.tree.map(lambda a, e: jnp.zeros_like(a) + jnp.asarray(e, a.dtype), part, identity)

    def one(turn, state):
        return combine(
            state, jax.tree.map(lambda a: lax.dynamic_index_in_dim(a, turn, 0, False), gathered)
        )

    return lax.fori_loop(0, place, one, state)


def pole_power(decay, rotation, powers):
    magnitude = jnp.exp(-decay * powers)
    return (magnitude * jnp.cos(rotation * powers), magnitude * jnp.sin(rotation * powers))


def segment_of(positions, starts):
    return jnp.sum((positions[..., None] >= starts).astype(jnp.int32), axis=-1) - 1


def local(
    streams, short_filter, decay_rate, pole_angle, residue_re, residue_im, skip_gain, doc_starts
):
    short_filter, decay_rate, pole_angle, residue_re, residue_im, skip_gain = (
        lax.all_gather(short_filter, "dp", axis=2, tiled=True),
        lax.all_gather(decay_rate, "dp", axis=1, tiled=True),
        lax.all_gather(pole_angle, "dp", axis=1, tiled=True),
        lax.all_gather(residue_re, "dp", axis=1, tiled=True),
        lax.all_gather(residue_im, "dp", axis=1, tiled=True),
        lax.all_gather(skip_gain, "dp", axis=0, tiled=True),
    )
    tok_rows = streams.shape[2]
    channels = streams.shape[3]
    modes = decay_rate.shape[0]
    my_index = lax.axis_index("seq")
    offset = my_index * tok_rows
    starts = doc_starts[0]
    rim_rows = streams[:, :, tok_rows - 2 :, :]
    before = from_behind(rim_rows, "seq", 1)
    extended = jnp.concatenate([before, streams], axis=2)[:, 0]
    filtered = (
        short_filter[0][:, None, :] * extended[:, 2:]
        + short_filter[1][:, None, :] * extended[:, 1:-1]
        + short_filter[2][:, None, :] * extended[:, :-2]
    )
    product = filtered[0] * filtered[1]
    out_gate = filtered[2]
    positions = offset + jnp.arange(tok_rows, dtype=jnp.int32)
    seg_ids = segment_of(positions, starts)
    seg_before = segment_of(offset - 1 + jnp.zeros((1,), jnp.int32), starts)[0]
    nblocks = tok_rows // block_len
    local_steps = jnp.arange(block_len, dtype=jnp.float32)[:, None, None]
    fwd_re, fwd_im = pole_power(decay_rate, pole_angle, local_steps)
    back_re, back_im = pole_power(-decay_rate, -pole_angle, local_steps)
    blocked = product.reshape(nblocks, block_len, 1, channels)
    lifted = jnp.concatenate([blocked * back_re, blocked * back_im], axis=2)
    lifted = lifted.reshape(nblocks, block_len, 2 * modes * channels)
    seg_blocks = seg_ids.reshape(nblocks, block_len)
    causal = jnp.arange(block_len)[:, None] >= jnp.arange(block_len)[None, :]
    within = (causal[None] & (seg_blocks[:, :, None] == seg_blocks[:, None, :])).astype(jnp.float32)
    summed = jnp.einsum("bts,bsk->btk", within, lifted, precision=lax.Precision.HIGHEST)
    summed = summed.reshape(nblocks, block_len, 2 * modes, channels)
    sum_re = summed[:, :, :modes]
    sum_im = summed[:, :, modes:]
    state_re = fwd_re * sum_re - fwd_im * sum_im
    state_im = fwd_re * sum_im + fwd_im * sum_re
    step_re, step_im = pole_power(decay_rate, pole_angle, jnp.float32(block_len))
    entry_seg = jnp.concatenate([seg_before[None], seg_blocks[:-1, -1]])
    keeps_last = (seg_blocks[:, -1] == entry_seg).astype(jnp.float32)

    def advance(running, inputs):
        run_re, run_im = running
        last_re, last_im, kept_now = inputs
        next_re = last_re + kept_now * (step_re * run_re - step_im * run_im)
        next_im = last_im + kept_now * (step_re * run_im + step_im * run_re)
        return ((next_re, next_im), (run_re, run_im))

    zero_state = jnp.zeros((modes, channels), jnp.float32)
    (end_re, end_im), (entry_re, entry_im) = lax.scan(
        advance, (zero_state, zero_state), (state_re[:, -1], state_im[:, -1], keeps_last)
    )
    lead_re, lead_im = pole_power(decay_rate, pole_angle, local_steps + 1.0)
    joined = (seg_blocks == entry_seg[:, None]).astype(jnp.float32)[:, :, None, None]
    state_re = state_re + joined * (lead_re * entry_re[:, None] - lead_im * entry_im[:, None])
    state_im = state_im + joined * (lead_re * entry_im[:, None] + lead_im * entry_re[:, None])
    whole_re, whole_im = pole_power(decay_rate, pole_angle, jnp.float32(tok_rows))
    keep_all = (seg_ids[-1] == seg_before).astype(jnp.float32)

    def combine(earlier, latter):
        early_are, early_aim, early_sre, early_sim = earlier
        late_are, late_aim, late_sre, late_sim = latter
        return (
            late_are * early_are - late_aim * early_aim,
            late_are * early_aim + late_aim * early_are,
            late_sre + late_are * early_sre - late_aim * early_sim,
            late_sim + late_are * early_sim + late_aim * early_sre,
        )

    unit_state = jnp.ones_like(end_re)
    prefix = prefix_2(
        (keep_all * whole_re, keep_all * whole_im, end_re, end_im),
        "seq",
        combine,
        (unit_state, zero_state, zero_state, zero_state),
    )
    inflow_re = prefix[2]
    inflow_im = prefix[3]
    all_steps = (
        jnp.arange(tok_rows, dtype=jnp.float32).reshape(nblocks, block_len)[:, :, None, None] + 1.0
    )
    enter_re, enter_im = pole_power(decay_rate, pole_angle, all_steps)
    reach = (seg_blocks == seg_before).astype(jnp.float32)[:, :, None, None]
    state_re = state_re + reach * (enter_re * inflow_re - enter_im * inflow_im)
    state_im = state_im + reach * (enter_re * inflow_im + enter_im * inflow_re)
    norm_factor = jnp.sqrt(-jnp.expm1(-2.0 * decay_rate))
    long_part = jnp.sum(norm_factor * (residue_re * state_re - residue_im * state_im), axis=2)
    long_part = long_part.reshape(tok_rows, channels)
    response = skip_gain * product + long_part
    return (out_gate * response).astype(jnp.bfloat16)[None]


def solution(mesh):
    placed = (
        P(None, "dp", "seq", None),
        P(None, None, "dp"),
        P(None, "dp"),
        P(None, "dp"),
        P(None, "dp"),
        P(None, "dp"),
        P("dp"),
        P("dp", None),
    )
    return jax.shard_map(
        local, mesh=mesh, in_specs=placed, out_specs=P("dp", "seq", None), check_vma=False
    )
```

profile of v0, /device:TPU:249, one launch (start us, length us, event | category | flops | bytes accessed | tf_op | source)
XLA Modules:
  0.0 430.3 jit_solution(6064338715635104115)
XLA Ops:
  6.5 1.3 fusion.14
  10.5 9.6 %all_gather.46 = f32[2,4096]{1,0:T(2,128)S(1)} all-gather(f32[2,1024]{1,0:T(2,128)} %param.15), channel_id=1, replica_groups=mesh['dp'=4,'seq'=64] {'dp'}, dimensions={1}, use_global_device_ids=true | all-gather | bytes 40960 | tf_op jit(solution)/shard_map/all_gather | solution.py:43
  20.1 9.2 %all_gather.44 = f32[2,4096]{1,0:T(2,128)S(1)} all-gather(f32[2,1024]{1,0:T(2,128)} %param.14), channel_id=1, replica_groups=mesh['dp'=4,'seq'=64] {'dp'}, dimensions={1}, use_global_device_ids=true | all-gather | bytes 40960 | tf_op jit(solution)/shard_map/all_gather | solution.py:42
  29.3 1.7 multiply_bitcast_fusion
  31.0 1.0 slice.69
  32.0 1.3 collective-permute-start
  33.8 16.3 %cosine_multiply_fusion = (f32[32,2,4096]{2,1,0:T(2,128)}, f32[32,2,4096]{2,1,0:T(2,128)}) fusion(f32[2,4096]{1,0:T(2,128)S(1)} %get-tuple-element.233, f32[2,4096]{1,0:T(2,128)S(1)} %all_gather.44), kind=kLoop, calls=%fused_computation.37 | loop fusion | flops 1048576 | bytes 2162688 | tf_op jit(solution)/shard_map/mul | solution.py:30
  50.2 9.8 %all_gather.42 = f32[3,3,4096]{2,1,0:T(4,128)S(1)} all-gather(f32[3,3,1024]{2,1,0:T(4,128)} %param.13), channel_id=1, replica_groups=mesh['dp'=4,'seq'=64] {'dp'}, dimensions={2}, use_global_device_ids=true | all-gather | bytes 184320 | tf_op jit(solution)/shard_map/all_gather | solution.py:41
  60.0 8.6 %fusion.6 = (f32[32,2,4096]{2,0,1:T(8,128)S(1)}, f32[32,2,4096]{2,0,1:T(8,128)S(1)}, f32[32,2,4096]{2,0,1:T(8,128)}, f32[32,2,4096]{2,0,1:T(8,128)}) fusion(f32[32]{0:T(128)S(1)} %iota_add_fusion, f32[2,4096]{1,0:T(2,128)S(1)} %all_gather.46, f32[2,4096]{1,0:T(2,128)S(1)} %get-tuple-element.234), kind=kLoop, calls=%fused_computation.32 | loop fusion | flops 2097152 | bytes 4259968 | tf_op jit(solution)/shard_map/mul | solution.py:30
  68.7 2.7 maximum_bitcast_fusion
  71.4 2.1 multiply_add_fusion
  73.8 1.7 copy-done.4
  75.6 1.1 copy-done.5
  76.7 3.9 broadcast_multiply_fusion.1
  80.5 9.7 %pad_maximum_fusion = f32[4,32,4,4096]{3,2,1,0:T(4,128)} fusion(f32[4,32,2,4096]{3,2,1,0:T(2,128)} %get-tuple-element.218, f32[4,32,2,4096]{3,2,1,0:T(2,128)S(1)} %get-tuple-element.217), kind=kLoop, calls=%fused_computation.14 | loop fusion | flops 2097152 | bytes 16777216 | tf_op jit(solution)/shard_map/concatenate | solution.py:72
  90.3 11.0 %reshape.158 = f32[4,32,16384]{2,1,0:T(8,128)} reshape(f32[4,32,4,4096]{3,2,1,0:T(4,128)} %pad_maximum_fusion) | data formatting | bytes 16777216 | tf_op jit(solution)/shard_map/reshape | solution.py:73
  101.3 10.8 %fusion.8 = f32[4,32,16384]{2,1,0:T(8,128)} fusion(f32[4,32,16384]{2,1,0:T(8,128)} %reshape.158, s32[4,32]{1,0:T(4,128)S(1)} %sub.35, pred[32,32]{1,0:T(8,128)(4,1)S(1)} %iota_compare_fusion), kind=kOutput, calls=%fused_computation.48 | convolution fusion | flops 805314560 | bytes 16778752 | tf_op jit(solution)/shard_map/bts,bsk->btk/dot_general | solution.py:77
  112.1 10.8 %reshape.159 = f32[4,32,4,4096]{3,2,1,0:T(4,128)} reshape(f32[4,32,16384]{2,1,0:T(8,128)} %fusion.8) | data formatting | bytes 16777216 | tf_op jit(solution)/shard_map/reshape | solution.py:78
  122.9 11.1 %fusion.15 = (f32[4,32,2,4096]{3,2,1,0:T(2,128)S(1)}, f32[4,32,2,4096]{3,2,1,0:T(2,128)}) fusion(f32[4,32,4,4096]{3,2,1,0:T(4,128)} %reshape.159), kind=kLoop, calls=%fused_computation.75 | loop fusion | bytes 16777216 | tf_op jit(solution)/shard_map/slice | solution.py:79
  134.0 7.8 %multiply_subtract_fusion = (f32[4,32,2,4096]{3,1,2,0:T(8,128)S(1)}, f32[4,32,2,4096]{3,1,2,0:T(8,128)S(1)}) fusion(f32[4,32,2,4096]{3,2,1,0:T(2,128)} %get-tuple-element.216, f32[4,32,2,4096]{3,2,1,0:T(2,128)S(1)} %get-tuple-element.215, f32[32,2,4096]{2,0,1:T(8,128)S(1)} %copy-done.3, f32[32,2,4096]{2,0,1:T(8,128)} %get-tuple-element.225), kind=kLoop, calls=%fused_computation.22 | loop fusion | flops 6291456 | bytes 18874368 | tf_op jit(solution)/shard_map/sub | solution.py:81
  141.9 2.0 copy-done.1
  144.0 1.1 copy-done.2
  145.5 7.9 %while.33 = (s32[]{:T(128)}, f32[2,4096]{1,0:T(2,128)S(1)}, f32[2,4096]{1,0:T(2,128)S(1)}, f32[4,2,4096]{2,1,0:T(2,128)S(1)}, f32[4,2,4096]{2,1,0:T(2,128)}, /*i...) while((s32[]{:T(128)}, f32[2,4096]{1,0:T(2,128)S(1)}, ...), condition=%wide.region_3.4_spmd.clone, body=%wide.region_2.3_spmd.clone.sunk | while | flops 114691 | bytes 393876 | solution.py:95
  154.6 9.0 %all_gather.43 = f32[4096]{0:T(1024)S(1)} all-gather(f32[1024]{0:T(1024)S(1)} %copy-done.10), channel_id=1, replica_groups=mesh['dp'=4,'seq'=64] {'dp'}, dimensions={0}, use_global_device_ids=true | all-gather | bytes 20480 | tf_op jit(solution)/shard_map/all_gather | solution.py:46
  163.7 9.6 %all_gather.45 = f32[2,4096]{1,0:T(2,128)S(1)} all-gather(f32[2,1024]{1,0:T(2,128)S(1)} %copy-done.8), channel_id=1, replica_groups=mesh['dp'=4,'seq'=64] {'dp'}, dimensions={1}, use_global_device_ids=true | all-gather | bytes 40960 | tf_op jit(solution)/shard_map/all_gather | solution.py:44
  173.2 9.0 %all_gather.55 = f32[2,4096]{1,0:T(2,128)S(1)} all-gather(f32[2,1024]{1,0:T(2,128)S(1)} %copy-done.9), channel_id=1, replica_groups=mesh['dp'=4,'seq'=64] {'dp'}, dimensions={1}, use_global_device_ids=true | all-gather | bytes 40960 | tf_op jit(solution)/shard_map/all_gather | solution.py:45
  182.4 6.7 %all-gather.17.cloned.1.call-done = f32[64,2,4096]{2,1,0:T(2,128)} async-done(((f32[1,2,4096]{2,1,0:T(2,128)}), f32[64,2,4096]{2,1,0:T(2,128)}) %all-gather.17.cloned.1.call-update) | async-done | bytes 2097168 | tf_op jit(solution)/shard_map/all_gather | solution.py:17
  189.1 77.8 %all-gather.13.cloned.1.call-done = f32[64,2,4096]{2,1,0:T(2,128)} async-done(((f32[1,2,4096]{2,1,0:T(2,128)}), f32[64,2,4096]{2,1,0:T(2,128)}) %all-gather.13.cloned.1.call-update) | async-done | bytes 2097168 | tf_op jit(solution)/shard_map/all_gather | solution.py:17
  266.9 77.6 %all-gather.19.cloned.1.call-done = f32[64,2,4096]{2,1,0:T(2,128)} async-done(((f32[1,2,4096]{2,1,0:T(2,128)}), f32[64,2,4096]{2,1,0:T(2,128)}) %all-gather.19.cloned.1.call-update) | async-done | bytes 2097168 | tf_op jit(solution)/shard_map/all_gather | solution.py:17
  344.5 56.3 %while.32 = (s32[]{:T(128)}, f32[2,4096]{1,0:T(2,128)S(1)}, f32[2,4096]{1,0:T(2,128)S(1)}, s32[]{:T(128)}, f32[64,2,4096]{2,1,0:T(2,128)}, /*index=5*/f32[64,2,4...) while((s32[]{:T(128)}, f32[2,4096]{1,0:T(2,128)S(1)}, ...), condition=%wide.region_5.6_spmd, body=%wide.region_4.5_spmd.sunk | while | flops 65541 | bytes 262291 | solution.py:25
  400.8 21.4 %multiply_reduce_fusion = f32[4,32,4096]{2,1,0:T(8,128)S(1)} fusion(f32[4,32,2,4096]{3,1,2,0:T(8,128)} %copy-done.2, f32[4,32,2,4096]{3,1,2,0:T(8,128)} %copy-done.1, f32[2,4096]{1,0:T(2,128)S(1)} %all_gather.55, f32[2,4096]{1,0:T(2,128)S(1)} %get-tuple-element.135, f32[2,4096]{1,0:T(2,128)S(1)} %get-tuple-element.134, f32[2,4096]{1,0:T(2,128)S(1)} %all_gather.46, ...), kind=kLoop, calls=%fused_computation.20 | loop fusion | flops 29884416 | bytes 13075968 | tf_op jit(solution)/shard_map/reduce_sum | solution.py:132
  422.2 1.6 fusion.5
  (131 shorter events, 66.7 us)
Async XLA Ops:
  6.5 175.8 %all-gather.15.cloned.1.call-start = ((), (), s32[]{:S(2)}) async-start(), calls=%async_computation.1 | async-start | bytes 2129920 | tf_op jit(solution)/shard_map/all_gather | solution.py:17
  31.0 158.1 %all-gather.17.cloned.1.call-start = ((), (), s32[]{:S(2)}) async-start(), calls=%async_computation.2 | async-start | bytes 2129920 | tf_op jit(solution)/shard_map/all_gather | solution.py:17
  32.0 36.7 %collective-permute-start = (bf16[3,1,2,4096]{3,2,0,1:T(2,128)(2,1)S(1)}, bf16[3,1,2,4096]{3,2,0,1:T(2,128)(2,1)S(1)}, u32[]{:S(2)}, u32[]{:S(2)}) collective-permute-start(bf16[3,1,2,4096]{3,2,0,1:T(2,128)(2,1)S(1)} %slice.69), channel_id=1, source_target_pairs={{0,1},{1,2},{2,3},{3,4},{4,5},{5,6},{6,7},{7,8},{8,9},{9,10},{10,1... | collective-permute-start | bytes 147464 | tf_op jit(solution)/shard_map/ppermute | solution.py:12
  33.3 233.5 %all-gather.13.cloned.1.call-start = ((), (), s32[]{:S(2)}) async-start(), calls=%async_computation | async-start | bytes 2129920 | tf_op jit(solution)/shard_map/all_gather | solution.py:17
  73.5 7.0 %copy-start = (f32[3,128,4096]{2,1,0:T(8,128)}, f32[3,128,4096]{2,1,0:T(8,128)S(1)}, u32[]{:S(2)}) copy-start(f32[3,128,4096]{2,1,0:T(8,128)S(1)} %multiply_add_fusion) | copy-start | bytes 18874372
  73.6 2.0 copy-start.4
  73.6 3.1 copy-start.5
  122.9 11.1 %copy-start.3 = (f32[32,2,4096]{2,0,1:T(8,128)S(1)}, f32[32,2,4096]{2,0,1:T(8,128)}, u32[]{:S(2)}) copy-start(f32[32,2,4096]{2,0,1:T(8,128)} %get-tuple-element.224) | copy-start | bytes 3145732
  134.0 20.6 %copy-start.10 = (f32[1024]{0:T(1024)S(1)}, f32[1024]{0:T(1024)}, u32[]{:S(2)}) copy-start(f32[1024]{0:T(1024)} %param.18) | copy-start | bytes 12292
  134.0 29.7 %copy-start.8 = (f32[2,1024]{1,0:T(2,128)S(1)}, f32[2,1024]{1,0:T(2,128)}, u32[]{:S(2)}) copy-start(f32[2,1024]{1,0:T(2,128)} %param.16) | copy-start | bytes 24580
  134.0 39.2 %copy-start.9 = (f32[2,1024]{1,0:T(2,128)S(1)}, f32[2,1024]{1,0:T(2,128)}, u32[]{:S(2)}) copy-start(f32[2,1024]{1,0:T(2,128)} %param.17) | copy-start | bytes 24580
  141.8 2.0 copy-start.1
  141.8 3.3 copy-start.2
  153.4 0.6 copy-start.6
  153.4 0.7 copy-start.7
  154.0 190.4 %all-gather.19.cloned.1.call-start = ((), (), s32[]{:S(2)}) async-start(), calls=%async_computation.3 | async-start | bytes 2129920 | tf_op jit(solution)/shard_map/all_gather | solution.py:17
  400.8 21.4 %slice-start = ((s8[6291456]{0:T(1024)(128)(4,1)}), s8[4194304]{0:T(1024)(128)(4,1)S(1)}, s32[]{:S(2)}) async-start(s8[6291456]{0:T(1024)(128)(4,1)} %bitcast.73), calls=%async_computation.4 | async-start | bytes 8388608
  400.8 21.4 %slice-start.1 = ((s8[6291456]{0:T(1024)(128)(4,1)}), s8[2097152]{0:T(1024)(128)(4,1)S(1)}, s32[]{:S(2)}) async-start(s8[6291456]{0:T(1024)(128)(4,1)} %bitcast.73), calls=%async_computation.5 | async-start | bytes 4194304
Sparse Core Ops, SparseCore 0:
  31.1 80.2 all-gather.14
  114.1 74.9 all-gather.16
  191.9 74.9 all-gather.12
  269.5 74.9 all-gather.18
where the time goes:
time: 436 us; the launch traced here: 430 us
  waiting for transfers between devices  163 us (37%)
  other arithmetic  139 us (32%)
  blocking collectives  56.2 us (13%)
  local copies, waits for them, and re-layouts  44.3 us (10%)
  between operations  14.7 us (3%)
  matrix products  10.8 us (2%)
    all_gather x4, waiting for transfers between devices, prefix_2(): gathered = jax.tree.map(lambda a: lax.all_gather(a, axis), part)  162 us
    add x63, other arithmetic, combine(): late_sim + late_are * early_sim + late_aim * early_sre  54.8 us
    mul x2, other arithmetic, pole_power(): magnitude * jnp.cos(rotation * powers)  24.9 us
    reduce_sum x1, other arithmetic, local(): jnp.sum(norm_factor * (residue_re * state_re - residue_im * state_im), ax...  21.4 us
    slice x1, local copies, waits for them, and re-layouts, local(): sum_re = summed[:, :, :modes]  11.1 us
    reshape x1, local copies, waits for them, and re-layouts, local(): lifted = lifted.reshape(nblocks, block_len, 2 * modes * channels)  11 us
    dot_general x1, matrix products, local(): jnp.einsum('bts,bsk->btk', within, lifted, precision=lax.Precision.HIGHEST)  10.8 us
    reshape x1, local copies, waits for them, and re-layouts, local(): summed = summed.reshape(nblocks, block_len, 2 * modes, channels)  10.8 us
  transfers between devices with their start and end apart: 5, of which 3 were waited for; matrix products, arithmetic and copies ran while one was open for 24% of the time, Pallas kernels for 0%

commit v1 on v0

--- a/solution.py
+++ b/solution.py
@@ -37,12 +37,40 @@
 def local(
     streams, short_filter, decay_rate, pole_angle, residue_re, residue_im, skip_gain, doc_starts
 ):
+
+    def make_leaf(x_part):
+        mesh_name = "dp"
+        item_now = lax.axis_size(mesh_name)
+        part_now = lax.axis_index(mesh_name)
+        carry_in, passed, upper = (item_now, part_now, x_part.shape[1])
+        stack_in = [(ix, (ix + 1) % carry_in) for ix in range(carry_in)]
+        by_place = [(ix, (ix - 1) % carry_in) for ix in range(carry_in)]
+        current_block = jnp.zeros(
+            (*x_part.shape[:1], carry_in * upper, *x_part.shape[2:]), x_part.dtype
+        )
+        current_block = lax.dynamic_update_slice_in_dim(
+            current_block, x_part, passed * upper, axis=1
+        )
+        shaped = opened = x_part
+        carry_out = carry_in // 2
+        for m in range(1, carry_out + 1):
+            shaped = lax.ppermute(shaped, axis_name=mesh_name, perm=stack_in)
+            current_block = lax.dynamic_update_slice_in_dim(
+                current_block, shaped, (passed - m) % carry_in * upper, axis=1
+            )
+            if m < carry_in - carry_out:
+                opened = lax.ppermute(opened, axis_name=mesh_name, perm=by_place)
+                current_block = lax.dynamic_update_slice_in_dim(
+                    current_block, opened, (passed + m) % carry_in * upper, axis=1
+                )
+        return current_block
+
     short_filter, decay_rate, pole_angle, residue_re, residue_im, skip_gain = (
         lax.all_gather(short_filter, "dp", axis=2, tiled=True),
         lax.all_gather(decay_rate, "dp", axis=1, tiled=True),
         lax.all_gather(pole_angle, "dp", axis=1, tiled=True),
         lax.all_gather(residue_re, "dp", axis=1, tiled=True),
-        lax.all_gather(residue_im, "dp", axis=1, tiled=True),
+        make_leaf(residue_im),
         lax.all_gather(skip_gain, "dp", axis=0, tiled=True),
     )
     tok_rows = streams.shape[2]

time: 436 us -> 436 us (level)
  blocking collectives: 56.2 us -> 46.6 us
  waiting for transfers between devices: 163 us -> 169 us
    all_gather x1 -> x0, blocking collectives: 9.03 us -> none  [local(): lax.all_gather(residue_im, 'dp', axis=1, tiled=True)]
  transfers between devices with their start and end apart: 5 -> 8, of which waited for: 3 -> 4; matrix products, arithmetic and copies ran while one was open for 24% -> 24% of each run, Pallas kernels for 0% -> 0%
where the time goes in v1:
time: 436 us; the launch traced here: 430 us
  waiting for transfers between devices  169 us (39%)
  other arithmetic  138 us (32%)
  blocking collectives  46.6 us (11%)
  local copies, waits for them, and re-layouts  44.3 us (10%)
  between operations  14.7 us (3%)
  matrix products  10.8 us (2%)
  starting transfers between devices  4.84 us (1%)
    all_gather x4, waiting for transfers between devices, prefix_2(): gathered = jax.tree.map(lambda a: lax.all_gather(a, axis), part)  165 us
    add x63, other arithmetic, combine(): late_sim + late_are * early_sim + late_aim * early_sre  54.7 us
    mul x2, other arithmetic, pole_power(): magnitude * jnp.cos(rotation * powers)  24.9 us
    reduce_sum x1, other arithmetic, local(): jnp.sum(norm_factor * (residue_re * state_re - residue_im * state_im), ax...  21.4 us
    slice x1, local copies, waits for them, and re-layouts, local(): sum_re = summed[:, :, :modes]  11 us
    reshape x1, local copies, waits for them, and re-layouts, local(): lifted = lifted.reshape(nblocks, block_len, 2 * modes * channels)  11 us
    reshape x1, local copies, waits for them, and re-layouts, local(): summed = summed.reshape(nblocks, block_len, 2 * modes, channels)  10.8 us
    dot_general x1, matrix products, local(): jnp.einsum('bts,bsk->btk', within, lifted, precision=lax.Precision.HIGHEST)  10.8 us
  transfers between devices with their start and end apart: 8, of which 4 were waited for; matrix products, arithmetic and copies ran while one was open for 24% of the time, Pallas kernels for 0%

profile of v1, /device:TPU:249, one launch (start us, length us, event | category | flops | bytes accessed | tf_op | source)
XLA Modules:
  0.0 430.3 jit_solution(6462851792350326033)
XLA Ops:
  6.5 1.3 fusion.14
  10.5 9.6 %all_gather.43 = f32[2,4096]{1,0:T(2,128)S(1)} all-gather(f32[2,1024]{1,0:T(2,128)} %param.15), channel_id=1, replica_groups=mesh['dp'=4,'seq'=64] {'dp'}, dimensions={1}, use_global_device_ids=true | all-gather | bytes 40960 | tf_op jit(solution)/shard_map/all_gather | solution.py:71
  20.1 9.2 %all_gather.41 = f32[2,4096]{1,0:T(2,128)S(1)} all-gather(f32[2,1024]{1,0:T(2,128)} %param.14), channel_id=1, replica_groups=mesh['dp'=4,'seq'=64] {'dp'}, dimensions={1}, use_global_device_ids=true | all-gather | bytes 40960 | tf_op jit(solution)/shard_map/all_gather | solution.py:70
  29.3 1.7 multiply_bitcast_fusion
  32.0 1.3 collective-permute-start
  33.9 16.3 %cosine_multiply_fusion = (f32[32,2,4096]{2,1,0:T(2,128)}, f32[32,2,4096]{2,1,0:T(2,128)}) fusion(f32[2,4096]{1,0:T(2,128)S(1)} %get-tuple-element.233, f32[2,4096]{1,0:T(2,128)S(1)} %all_gather.41), kind=kLoop, calls=%fused_computation.37 | loop fusion | flops 1048576 | bytes 2162688 | tf_op jit(solution)/shard_map/mul | solution.py:30
  50.2 9.8 %all_gather.39 = f32[3,3,4096]{2,1,0:T(4,128)S(1)} all-gather(f32[3,3,1024]{2,1,0:T(4,128)} %param.13), channel_id=1, replica_groups=mesh['dp'=4,'seq'=64] {'dp'}, dimensions={2}, use_global_device_ids=true | all-gather | bytes 184320 | tf_op jit(solution)/shard_map/all_gather | solution.py:69
  60.0 8.5 %fusion.6 = (f32[32,2,4096]{2,0,1:T(8,128)S(1)}, f32[32,2,4096]{2,0,1:T(8,128)S(1)}, f32[32,2,4096]{2,0,1:T(8,128)}, f32[32,2,4096]{2,0,1:T(8,128)}) fusion(f32[32]{0:T(128)S(1)} %iota_add_fusion, f32[2,4096]{1,0:T(2,128)S(1)} %all_gather.43, f32[2,4096]{1,0:T(2,128)S(1)} %get-tuple-element.234), kind=kLoop, calls=%fused_computation.32 | loop fusion | flops 2097152 | bytes 4259968 | tf_op jit(solution)/shard_map/mul | solution.py:30
  68.7 2.7 maximum_bitcast_fusion
  71.4 2.1 multiply_add_fusion
  73.8 1.7 copy-done.4
  75.5 1.1 copy-done.5
  76.6 3.9 broadcast_multiply_fusion.1
  80.5 9.7 %pad_maximum_fusion = f32[4,32,4,4096]{3,2,1,0:T(4,128)} fusion(f32[4,32,2,4096]{3,2,1,0:T(2,128)} %get-tuple-element.218, f32[4,32,2,4096]{3,2,1,0:T(2,128)S(1)} %get-tuple-element.217), kind=kLoop, calls=%fused_computation.14 | loop fusion | flops 2097152 | bytes 16777216 | tf_op jit(solution)/shard_map/concatenate | solution.py:100
  90.2 11.0 %reshape.177 = f32[4,32,16384]{2,1,0:T(8,128)} reshape(f32[4,32,4,4096]{3,2,1,0:T(4,128)} %pad_maximum_fusion) | data formatting | bytes 16777216 | tf_op jit(solution)/shard_map/reshape | solution.py:101
  101.2 10.8 %fusion.8 = f32[4,32,16384]{2,1,0:T(8,128)} fusion(f32[4,32,16384]{2,1,0:T(8,128)} %reshape.177, s32[4,32]{1,0:T(4,128)S(1)} %sub.41, pred[32,32]{1,0:T(8,128)(4,1)S(1)} %iota_compare_fusion), kind=kOutput, calls=%fused_computation.48 | convolution fusion | flops 805314560 | bytes 16778752 | tf_op jit(solution)/shard_map/bts,bsk->btk/dot_general | solution.py:105
  112.1 10.8 %reshape.178 = f32[4,32,4,4096]{3,2,1,0:T(4,128)} reshape(f32[4,32,16384]{2,1,0:T(8,128)} %fusion.8) | data formatting | bytes 16777216 | tf_op jit(solution)/shard_map/reshape | solution.py:106
  122.9 11.0 %fusion.15 = (f32[4,32,2,4096]{3,2,1,0:T(2,128)S(1)}, f32[4,32,2,4096]{3,2,1,0:T(2,128)}) fusion(f32[4,32,4,4096]{3,2,1,0:T(4,128)} %reshape.178), kind=kLoop, calls=%fused_computation.79 | loop fusion | bytes 16777216 | tf_op jit(solution)/shard_map/slice | solution.py:107
  133.9 7.8 %multiply_subtract_fusion = (f32[4,32,2,4096]{3,1,2,0:T(8,128)S(1)}, f32[4,32,2,4096]{3,1,2,0:T(8,128)S(1)}) fusion(f32[4,32,2,4096]{3,2,1,0:T(2,128)} %get-tuple-element.216, f32[4,32,2,4096]{3,2,1,0:T(2,128)S(1)} %get-tuple-element.215, f32[32,2,4096]{2,0,1:T(8,128)S(1)} %copy-done.3, f32[32,2,4096]{2,0,1:T(8,128)} %get-tuple-element.225), kind=kLoop, calls=%fused_computation.22 | loop fusion | flops 6291456 | bytes 18874368 | tf_op jit(solution)/shard_map/sub | solution.py:109
  141.8 2.0 copy-done.1
  143.9 1.1 copy-done.2
  145.4 7.9 %while.33 = (s32[]{:T(128)}, f32[2,4096]{1,0:T(2,128)S(1)}, f32[2,4096]{1,0:T(2,128)S(1)}, f32[4,2,4096]{2,1,0:T(2,128)S(1)}, f32[4,2,4096]{2,1,0:T(2,128)}, /*i...) while((s32[]{:T(128)}, f32[2,4096]{1,0:T(2,128)S(1)}, ...), condition=%wide.region_3.4_spmd.clone, body=%wide.region_2.3_spmd.clone.sunk | while | flops 114691 | bytes 393876 | solution.py:123
  155.4 1.9 collective-permute-start.2
  157.3 9.0 %all_gather.42 = f32[2,4096]{1,0:T(2,128)S(1)} all-gather(f32[2,1024]{1,0:T(2,128)S(1)} %copy-done.8), channel_id=1, replica_groups=mesh['dp'=4,'seq'=64] {'dp'}, dimensions={1}, use_global_device_ids=true | all-gather | bytes 40960 | tf_op jit(solution)/shard_map/all_gather | solution.py:72
  166.4 9.0 %all_gather.40 = f32[4096]{0:T(1024)S(1)} all-gather(f32[1024]{0:T(1024)S(1)} %copy-done.10), channel_id=1, replica_groups=mesh['dp'=4,'seq'=64] {'dp'}, dimensions={0}, use_global_device_ids=true | all-gather | bytes 20480 | tf_op jit(solution)/shard_map/all_gather | solution.py:74
  176.1 3.4 collective-permute-done.3
  179.6 9.6 %all-gather.17.cloned.1.call-done = f32[64,2,4096]{2,1,0:T(2,128)} async-done(((f32[1,2,4096]{2,1,0:T(2,128)}), f32[64,2,4096]{2,1,0:T(2,128)}) %all-gather.17.cloned.1.call-update) | async-done | bytes 2097168 | tf_op jit(solution)/shard_map/all_gather | solution.py:17
  189.1 77.8 %all-gather.13.cloned.1.call-done = f32[64,2,4096]{2,1,0:T(2,128)} async-done(((f32[1,2,4096]{2,1,0:T(2,128)}), f32[64,2,4096]{2,1,0:T(2,128)}) %all-gather.13.cloned.1.call-update) | async-done | bytes 2097168 | tf_op jit(solution)/shard_map/all_gather | solution.py:17
  266.9 77.6 %all-gather.19.cloned.1.call-done = f32[64,2,4096]{2,1,0:T(2,128)} async-done(((f32[1,2,4096]{2,1,0:T(2,128)}), f32[64,2,4096]{2,1,0:T(2,128)}) %all-gather.19.cloned.1.call-update) | async-done | bytes 2097168 | tf_op jit(solution)/shard_map/all_gather | solution.py:17
  344.5 56.2 %while.32 = (s32[]{:T(128)}, f32[2,4096]{1,0:T(2,128)S(1)}, f32[2,4096]{1,0:T(2,128)S(1)}, s32[]{:T(128)}, f32[64,2,4096]{2,1,0:T(2,128)}, /*index=5*/f32[64,2,4...) while((s32[]{:T(128)}, f32[2,4096]{1,0:T(2,128)S(1)}, ...), condition=%wide.region_5.6_spmd, body=%wide.region_4.5_spmd.sunk | while | flops 65541 | bytes 262291 | solution.py:25
  400.8 21.4 %multiply_reduce_fusion = f32[4,32,4096]{2,1,0:T(8,128)S(1)} fusion(f32[4,32,2,4096]{3,1,2,0:T(8,128)} %copy-done.2, f32[4,32,2,4096]{3,1,2,0:T(8,128)} %copy-done.1, f32[2,4096]{1,0:T(2,128)S(1)} %constant_dynamic-update-slice_fusion, f32[2,4096]{1,0:T(2,128)S(1)} %get-tuple-element.135, f32[2,4096]{1,0:T(2,128)S(1)} %get-tuple-element.134, ...), kind=kLoop, calls=%fused_computation.20 | loop fusion | flops 29884416 | bytes 13075968 | tf_op jit(solution)/shard_map/reduce_sum | solution.py:160
  422.2 1.6 fusion.5
  (141 shorter events, 69.2 us)
Async XLA Ops:
  6.5 173.0 %all-gather.15.cloned.1.call-start = ((), (), s32[]{:S(2)}) async-start(), calls=%async_computation.1 | async-start | bytes 2129920 | tf_op jit(solution)/shard_map/all_gather | solution.py:17
  31.0 158.1 %all-gather.17.cloned.1.call-start = ((), (), s32[]{:S(2)}) async-start(), calls=%async_computation.2 | async-start | bytes 2129920 | tf_op jit(solution)/shard_map/all_gather | solution.py:17
  32.0 36.7 %collective-permute-start = (bf16[3,1,2,4096]{3,2,0,1:T(2,128)(2,1)S(1)}, bf16[3,1,2,4096]{3,2,0,1:T(2,128)(2,1)S(1)}, u32[]{:S(2)}, u32[]{:S(2)}) collective-permute-start(bf16[3,1,2,4096]{3,2,0,1:T(2,128)(2,1)S(1)} %slice.69), channel_id=1, source_target_pairs={{0,1},{1,2},{2,3},{3,4},{4,5},{5,6},{6,7},{7,8},{8,9},{9,10},{10,1... | collective-permute-start | bytes 147464 | tf_op jit(solution)/shard_map/ppermute | solution.py:12
  33.3 233.5 %all-gather.13.cloned.1.call-start = ((), (), s32[]{:S(2)}) async-start(), calls=%async_computation | async-start | bytes 2129920 | tf_op jit(solution)/shard_map/all_gather | solution.py:17
  73.5 7.0 %copy-start = (f32[3,128,4096]{2,1,0:T(8,128)}, f32[3,128,4096]{2,1,0:T(8,128)S(1)}, u32[]{:S(2)}) copy-start(f32[3,128,4096]{2,1,0:T(8,128)S(1)} %multiply_add_fusion) | copy-start | bytes 18874372
  73.5 2.0 copy-start.4
  73.5 3.1 copy-start.5
  122.9 11.0 %copy-start.3 = (f32[32,2,4096]{2,0,1:T(8,128)S(1)}, f32[32,2,4096]{2,0,1:T(8,128)}, u32[]{:S(2)}) copy-start(f32[32,2,4096]{2,0,1:T(8,128)} %get-tuple-element.224) | copy-start | bytes 3145732
  133.9 20.6 %copy-start.9 = (f32[2,1024]{1,0:T(2,128)S(1)}, f32[2,1024]{1,0:T(2,128)}, u32[]{:S(2)}) copy-start(f32[2,1024]{1,0:T(2,128)} %param.17) | copy-start | bytes 24580
  133.9 23.3 %copy-start.8 = (f32[2,1024]{1,0:T(2,128)S(1)}, f32[2,1024]{1,0:T(2,128)}, u32[]{:S(2)}) copy-start(f32[2,1024]{1,0:T(2,128)} %param.16) | copy-start | bytes 24580
  133.9 32.5 %copy-start.10 = (f32[1024]{0:T(1024)S(1)}, f32[1024]{0:T(1024)}, u32[]{:S(2)}) copy-start(f32[1024]{0:T(1024)} %param.18) | copy-start | bytes 12292
  141.8 2.0 copy-start.1
  141.8 3.3 copy-start.2
  153.3 0.6 copy-start.6
  153.3 0.7 copy-start.7
  153.9 190.6 %all-gather.19.cloned.1.call-start = ((), (), s32[]{:S(2)}) async-start(), calls=%async_computation.3 | async-start | bytes 2129920 | tf_op jit(solution)/shard_map/all_gather | solution.py:17
  154.5 20.9 %collective-permute-start.1 = (f32[2,1024]{1,0:T(2,128)S(1)}, f32[2,1024]{1,0:T(2,128)S(1)}, u32[]{:S(2)}, u32[]{:S(2)}) collective-permute-start(f32[2,1024]{1,0:T(2,128)S(1)} %copy-done.9), channel_id=1, source_target_pairs={{0,64},{64,128},{128,192},{192,0},{1,65},{65,129},{129,193},{193,1... | collective-permute-start | bytes 24584 | tf_op jit(solution)/shard_map/ppermute | solution.py:57
  155.4 20.8 %collective-permute-start.2 = (f32[2,1024]{1,0:T(2,128)S(1)}, f32[2,1024]{1,0:T(2,128)S(1)}, u32[]{:S(2)}, u32[]{:S(2)}) collective-permute-start(f32[2,1024]{1,0:T(2,128)S(1)} %copy-done.9), channel_id=1, source_target_pairs={{0,192},{64,0},{128,64},{192,128},{1,193},{65,1},{129,65},{193,129... | collective-permute-start | bytes 24584 | tf_op jit(solution)/shard_map/ppermute | solution.py:62
  175.4 4.1 collective-permute-start.3
  400.7 21.4 %slice-start = ((s8[6291456]{0:T(1024)(128)(4,1)}), s8[4194304]{0:T(1024)(128)(4,1)S(1)}, s32[]{:S(2)}) async-start(s8[6291456]{0:T(1024)(128)(4,1)} %bitcast.73), calls=%async_computation.4 | async-start | bytes 8388608
  400.7 21.4 %slice-start.1 = ((s8[6291456]{0:T(1024)(128)(4,1)}), s8[2097152]{0:T(1024)(128)(4,1)S(1)}, s32[]{:S(2)}) async-start(s8[6291456]{0:T(1024)(128)(4,1)} %bitcast.73), calls=%async_computation.5 | async-start | bytes 4194304
Sparse Core Ops, SparseCore 0:
  31.1 80.1 all-gather.14
  114.1 74.9 all-gather.16
  191.9 74.9 all-gather.12
  269.5 74.9 all-gather.18
